TPU v7x, 512 devices: a whole 4x4x16 slice. The times are simulated.
512 devices in a mesh: row: 16 (over x, z_hi, core), col: 32 (over z_lo, y).
Axes of the slice: x: 4, y: 4, z: 16 (z_hi: 2, z_lo: 8; z = z_hi * 8 + z_lo), core: 2. Of those that a mesh axis runs over, the one named last changes fastest.
Arguments:
- kernel: float32 [16384, 16384], P('row', 'col'), may hold values from 0 to 20, as said below
Outputs:
- factored: float32 [16384, 16384], P('row', 'col')
Inputs may be any that keep to these rules, and one draw needn't show every extreme that they name: `kernel`: in logical order K is symmetric and positive definite.
All inputs are finite; a program needn't handle non-finite values.
Results may differ from a plain program's by a relative error of at most 0.0003.
Values sent between devices are 32-bit elements; how exact they have to be, the bound alone decides.
A program may use at most 64 MiB of HBM per device.

v0:
```python
import jax
import jax.numpy as jnp
from jax import lax
from jax.experimental import pallas as pl
from jax.experimental.pallas import tpu as pltpu
from jax.sharding import PartitionSpec as P

NB = 512
B = 128
KROWS = 10 * B
UNITS = [(i, j) for i in range(4) for j in range(i, 4)]
KCH = 64
ACH = 32
NA = 1024 // ACH
LAG = 4
TOKEN, CROSS, LAND = 7, 15, 28
EARLY, FIRST = 14, 30
F32 = jnp.float32


HI = lax.Precision.HIGHEST


def lane(v, k):
    return jnp.take_along_axis(v, jnp.full((8, B), k, jnp.int32), axis=1)

def sub(v, i):
    return jnp.broadcast_to(v[i:i + 1, :], (8, B))

def micro(d, e):
    n = len(d)
    iota = lax.broadcasted_iota(jnp.int32, (8, B), 0)
    us, vs = [], []
    for s in range(n):
        j0 = 8 * s
        cols = [lane(d[s], j0 + k) for k in range(8)]
        sp = {(i, k): sub(cols[k], i) for k in range(8) for i in range(k + 1)}
        m = {}
        rec = []
        mcol = []
        dvec = sp[0, 0]
        for j in range(8):
            r = 1.0 / sp[j, j]
            rec.append(r)
            if j:
                dvec = jnp.where(iota == j, sp[j, j], dvec)
            f = {i: sp[j, i] * r for i in range(j + 1, 8)}
            fv = jnp.where(iota > j, cols[j] * r, 0.0)
            for k in range(j + 1, 8):
                cols[k] = cols[k] - fv * sp[j, k]
            for k in range(j):
                mcol[k] = mcol[k] - fv * m[j, k]
            mcol.append(jnp.where(iota == j, 1.0, -fv))
            for i in range(j + 1, 8):
                for k in range(i, 8):
                    sp[i, k] = sp[i, k] - f[i] * sp[j, k]
                for k in range(j):
                    m[i, k] = m[i, k] - f[i] * m[j, k]
                m[i, j] = -f[i]
        def apply(v):
            t = [mcol[k] * sub(v, k) for k in range(8)]
            while len(t) > 1:
                t = [t[i] + t[i + 1] for i in range(0, len(t), 2)]
            return t[0]
        z, w = apply(d[s]), apply(e[s])
        rs = lax.rsqrt(dvec)
        us.append(z * rs)
        vs.append(w * rs)
        zr = [sub(z, k) * rec[k] for k in range(8)]
        wr = [sub(w, k) * rec[k] for k in range(8)]
        for t in range(s + 1, n):
            qs = [lane(d[t], j0 + k) for k in range(8)]
            for k in range(8):
                yk = qs[k]
                for l in range(k):
                    yk = yk + m[k, l] * qs[l]
                d[t] = d[t] - yk * zr[k]
                e[t] = e[t] - yk * wr[k]
    return us, vs

def dot(a, b):
    return jnp.dot(a, b, precision=HI, preferred_element_type=F32)


def dot_t(a, b):
    return lax.dot_general(a, b, (((1,), (1,)), ((), ())), precision=HI, preferred_element_type=F32)


def tdot(a, b):
    return lax.dot_general(a, b, (((0,), (0,)), ((), ())), precision=HI, preferred_element_type=F32)

def factor(k_ref, u_ref, x_ref, w_ref):
    for n, (i, j) in enumerate(UNITS):
        w_ref[B * i:B * i + B, B * j:B * j + B] = k_ref[B * n:B * n + B, :]
    x_ref[...] = jnp.zeros((NB, NB), F32)
    u_ref[...] = jnp.zeros((NB, NB), F32)
    row = lax.broadcasted_iota(jnp.int32, (8, B), 0)
    col = lax.broadcasted_iota(jnp.int32, (8, B), 1)
    for k in range(4):
        o = B * k
        d = [w_ref[o + 8 * t:o + 8 * t + 8, o:o + B] for t in range(16)]
        e = [jnp.where(col == row + 8 * t, 1.0, 0.0) for t in range(16)]
        us, vs = micro(d, e)
        for t in range(16):
            u_ref[o + 8 * t:o + 8 * t + 8, o:o + B] = jnp.where(col >= row + 8 * t, us[t], 0.0)
            x_ref[o + 8 * t:o + 8 * t + 8, o:o + B] = vs[t]
        li = x_ref[o:o + B, o:o + B]
        if k:
            x_ref[o:o + B, :o] = jnp.dot(li, x_ref[o:o + B, :o], precision=HI, preferred_element_type=F32)
        if k < 3:
            u = jnp.dot(li, w_ref[o:o + B, o + B:], precision=HI, preferred_element_type=F32)
            u_ref[o:o + B, o + B:] = u
            w_ref[o + B:, o + B:] = w_ref[o + B:, o + B:] - tdot(u, u)
            x_ref[o + B:, :o + B] = x_ref[o + B:, :o + B] - tdot(u, x_ref[o:o + B, :o + B])


def comm_kernel(
    g_ref, k_out, ap_out, aq_out, kbuf, ap, aq,
    lsem, ksend, krecv, asend, arecv, q1s, q1r, q2s, q2r, q3s, q3r, tok,
):
    r = lax.axis_index("row")
    q = lax.axis_index("col")
    x, zh, c = r // 4, (r // 2) % 2, r % 2
    zl, y = q // 4, q % 4
    z = zh * 8 + zl

    def dev(dx=0, dy=0, dz=0, dc=0):
        xx, yy, zz = (x + dx) % 4, (y + dy) % 4, (z + dz) % 16
        cc = (c + dc) % 2
        return {"row": xx * 4 + (zz // 8) * 2 + cc, "col": (zz % 8) * 4 + yy}

    ids = {}

    def near(**d):
        key = tuple(sorted((k, v) for k, v in d.items() if v))
        if key not in ids:
            ids[key] = dev(**d)
        return ids[key]

    group = [(dx, dc) for dx in range(4) for dc in range(2) if dx or dc]
    partners = [dict(dy=1), dict(dy=2), dict(dy=3), dict(dz=1), dict(dz=2), dict(dz=14), dict(dz=15)]
    partners += [dict(dx=dx, dc=dc) for dx, dc in group]
    for p in partners + [dict(dz=8)]:
        near(**p)
    barrier = pltpu.get_barrier_semaphore()
    for p in partners:
        pl.semaphore_signal(barrier, inc=1, device_id=near(**p), device_id_type=pl.DeviceIdType.MESH)

    kroot = (r == 0) & (q == 0)
    locals_k = [
        pltpu.make_async_copy(
            g_ref.at[pl.ds(B * i, B), pl.ds(B * j, B)], kbuf.at[pl.ds(B * n, B)], lsem.at[n]
        )
        for n, (i, j) in enumerate(UNITS)
    ]
    local_a = pltpu.make_async_copy(g_ref, ap, lsem.at[10])
    local_q = pltpu.make_async_copy(g_ref.at[pl.ds(0, NB)], aq, lsem.at[11])

    @pl.when(kroot)
    def _():
        for cp in locals_k:
            cp.start()

    @pl.when(q == 0)
    def _():
        local_a.start()

    @pl.when(r == 0)
    def _():
        local_q.start()

    pl.semaphore_wait(barrier, len(partners))

    @pl.when(kroot)
    def _():
        for cp in locals_k:
            cp.wait()

    @pl.when(q == 0)
    def _():
        local_a.wait()

    @pl.when(r == 0)
    def _():
        local_q.wait()

    def remote(ref, ssem, rsem, d):
        return pltpu.make_async_remote_copy(
            src_ref=ref, dst_ref=ref, send_sem=ssem, recv_sem=rsem,
            device_id=near(**d), device_id_type=pl.DeviceIdType.MESH,
        )

    pos = {"x": x, "y": y, "z": z}
    k_trees = []
    for order in ("xyz", "yzx", "zxy"):
        children = []
        for k, d in enumerate(order):
            head = c == 0
            for e in order[k + 1:]:
                head = head & (pos[e] == 0)
            v = pos[d]
            if d == "z":
                even = head & (v % 2 == 0)
                children.append((even & (v < 8), dict(dz=2)))
                children.append((even & (v < 8), dict(dz=1)))
                children.append((even & ((v == 0) | (v > 10)), dict(dz=14)))
                children.append((even & ((v == 0) | (v > 8)), dict(dz=15)))
            else:
                children += [(head & (v == 0), {"d" + d: n}) for n in (2, 1, 3)]
        children.append((c == 0, {"dc": 1}))
        k_trees.append(children)

    def k_chunk(ch):
        return kbuf.at[pl.ds(KCH * ch, KCH)]

    def k_round(s):
        for t in range(3):
            ch = 3 * s + t
            if ch >= KROWS // KCH:
                continue

            @pl.when(jnp.logical_not(kroot))
            def _():
                remote(k_chunk(ch), ksend.at[ch, 0], krecv.at[ch], {"dc": 1}).wait_recv()

            for n, (cond, d) in enumerate(k_trees[t]):
                @pl.when(cond)
                def _():
                    remote(k_chunk(ch), ksend.at[ch, n], krecv.at[ch], d).start()

    def q_piece(e):
        return aq.at[pl.ds(64 * e, 64)]

    mine = x * 2 + c

    @pl.when(r == 0)
    def _():
        for n, (dx, dc) in enumerate(group):
            remote(q_piece(dx * 2 + dc), q1s.at[n], q1r, dict(dx=dx, dc=dc)).start()

    def gather(n, dx, dc):
        to_source = (zh == 0) & ((x + dx) % 4 == 0) & ((c + dc) % 2 == 0)
        return jnp.logical_not(to_source), remote(
            q_piece(mine), q3s.at[n], q3r.at[mine], dict(dx=dx, dc=dc)
        )

    def q_cross():
        @pl.when(r != 0)
        def _():
            remote(q_piece(mine), q1s.at[0], q1r, dict(dc=1)).wait_recv()

        pl.semaphore_wait(tok.at[7], 1)
        remote(q_piece(mine), q2s, q2r, dict(dz=8)).start()
        for n, (dx, dc) in enumerate(group):
            cond, cp = gather(n, dx, dc)

            @pl.when(cond)
            def _():
                cp.start()

    def q_land():
        pl.semaphore_wait(tok.at[7], 1)
        remote(q_piece(mine), q2s, q2r, dict(dz=8)).wait_recv()
        for n, (dx, dc) in enumerate(group):
            gather(n, dx, dc)[1].start()

    def token(n):
        @pl.when(n > 0)
        def _():
            pl.semaphore_wait(tok.at[jnp.maximum(n - 1, 0)], 1)

        pl.semaphore_signal(
            tok.at[n], inc=1, device_id=near(dz=15), device_id_type=pl.DeviceIdType.MESH
        )

    a_trees = [
        [
            ((y == 0) & (zl < 7), dict(dz=1)),
            ((y == 0) & (zl >= 1), dict(dy=1)),
            (((y == 0) | (y == 3)) & (zl >= 1), dict(dy=3)),
            ((zl == 1) & (y != 0), dict(dz=15)),
        ],
        [
            ((y == 1) & (zl < 7), dict(dz=1)),
            (((y == 0) & (zl == 0)) | (y == 1) | (y == 2), dict(dy=1)),
            ((y == 1) & (zl >= 1), dict(dy=3)),
        ],
        [
            (((y == 3) | (y == 2)) & (zl < 7), dict(dz=1)),
            ((y == 3) & (zl >= 1), dict(dy=1)),
            (((y == 0) & (zl == 0)) | ((y == 3) & (zl == 0)) | (y == 2), dict(dy=3)),
        ],
    ]

    def a_chunk(ch):
        return ap.at[pl.ds(pl.multiple_of(ACH * ch, ACH), ACH)]

    def pick(options):
        value = options[-1][1]
        for cond, v in reversed(options[:-1]):
            value = jnp.where(cond, v, value)
        return value

    depths = [
        pick([((y == 0), zl), ((zl == 0) & (y == 2), 4), (zl == 0, 3), (y == 2, zl + 2), (True, zl + 1)]),
        pick([((y == 0) & (zl == 0), 0), (y == 1, zl + 1), (y == 3, zl + 3), (True, zl + 2)]),
        pick([((y == 0) & (zl == 0), 0), (y == 3, zl + 1), (y == 1, zl + 3), (True, zl + 2)]),
    ]

    def a_step(g, carry):
        for t in range(3):
            k = g - LAG * depths[t]
            ch = 3 * k + t

            @pl.when((k >= 0) & (ch < NA))
            def _():
                @pl.when(q != 0)
                def _():
                    remote(a_chunk(ch), asend.at[ch, 0], arecv.at[ch], dict(dy=1)).wait_recv()

                for n, (cond, d) in enumerate(a_trees[t]):
                    @pl.when(cond)
                    def _():
                        remote(a_chunk(ch), asend.at[ch, n], arecv.at[ch], d).start()

        @pl.when((g >= TOKEN) & (g < TOKEN + 8))
        def _():
            token(g - TOKEN)

        @pl.when((g == CROSS) & (zh == 0))
        def _():
            q_cross()

        @pl.when((g == LAND) & (zh == 1))
        def _():
            q_land()

        return carry

    chunks = -(-NA // 3)
    steps = max(chunks + 10 * LAG, LAND + 1)
    far = jnp.minimum(x, 4 - x) + jnp.minimum(y, 4 - y) + jnp.minimum(z, 16 - z)
    early = FIRST + (far * EARLY) // 8
    lax.fori_loop(0, early, a_step, 0)
    rounds = -(-(KROWS // KCH) // 3)
    for s in range(rounds):
        k_round(s)
        a_step(early + s, 0)

    lax.fori_loop(early + rounds, steps, a_step, 0)

    for n, (dx, dc) in enumerate(group):
        e = ((x + dx) % 4) * 2 + (c + dc) % 2
        cond, cp = gather(n, dx, dc)

        @pl.when(r != 0)
        def _():
            remote(q_piece(e), q3s.at[n], q3r.at[e], dict(dc=1)).wait_recv()

        @pl.when(cond)
        def _():
            cp.wait_send()

        @pl.when(r == 0)
        def _():
            remote(q_piece(dx * 2 + dc), q1s.at[n], q1r, dict(dx=dx, dc=dc)).wait_send()

    @pl.when(zh == 0)
    def _():
        remote(q_piece(mine), q2s, q2r, dict(dz=8)).wait_send()

    for ch in range(KROWS // KCH):
        for n, (cond, d) in enumerate(k_trees[ch % 3]):
            @pl.when(cond)
            def _():
                remote(k_chunk(ch), ksend.at[ch, n], krecv.at[ch], d).wait_send()

    def a_drain(k, carry):
        for t in range(3):
            ch = 3 * k + t

            @pl.when(ch < NA)
            def _():
                for n, (cond, d) in enumerate(a_trees[t]):
                    @pl.when(cond)
                    def _():
                        remote(a_chunk(ch), asend.at[ch, n], arecv.at[ch], d).wait_send()

        return carry

    lax.fori_loop(0, chunks, a_drain, 0)

    outs = [
        pltpu.make_async_copy(src, dst, lsem.at[n])
        for n, (src, dst) in enumerate([(kbuf, k_out), (ap, ap_out), (aq, aq_out)])
    ]
    for cp in outs:
        cp.start()
    for cp in outs:
        cp.wait()


def distribute(kernel):
    dma, vmem = pltpu.SemaphoreType.DMA, pltpu.VMEM
    square = (NB, NB)
    return pl.pallas_call(
        comm_kernel,
        out_shape=[
            jax.ShapeDtypeStruct((KROWS, B), F32),
            jax.ShapeDtypeStruct((2 * NB, NB), F32),
            jax.ShapeDtypeStruct(square, F32),
        ],
        in_specs=[pl.BlockSpec(memory_space=pl.ANY)],
        out_specs=[pl.BlockSpec(memory_space=pl.ANY)] * 3,
        scratch_shapes=[
            vmem((KROWS, B), F32), vmem((2 * NB, NB), F32), vmem(square, F32),
            dma((12,)),
            dma((KROWS // KCH, 11)), dma((KROWS // KCH,)),
            dma((NA, 4)), dma((NA,)),
            dma((7,)), dma(()),
            dma(()), dma(()),
            dma((7,)), dma((8,)),
            pltpu.SemaphoreType.REGULAR((8,)),
        ],
        compiler_params=pltpu.CompilerParams(collective_id=0, has_side_effects=True),
        name="distribute",
    )(kernel)


def update_kernel(k_any, a_any, q_any, g_any, o_ref, kbuf, ap, aq, u_ref, x_ref, w_ref, pq, sems):
    r = lax.axis_index("row")
    q = lax.axis_index("col")
    loads = [
        pltpu.make_async_copy(src, dst, sems.at[n])
        for n, (src, dst) in enumerate([(k_any, kbuf), (a_any, ap), (q_any, aq), (g_any, o_ref)])
    ]
    for cp in loads:
        cp.start()
    loads[0].wait()
    factor(kbuf, u_ref, x_ref, w_ref)
    loads[1].wait()
    loads[2].wait()
    loads[3].wait()

    half = NB // 2
    pq[:half] = dot(x_ref[:half, :half], aq[:half, :])
    pq[half:] = dot(x_ref[half:, :], aq[...])
    rows = 256

    def body(n, carry):
        sl = pl.ds(pl.multiple_of(rows * n, rows), rows)
        a = ap[sl, :]
        p = jnp.concatenate(
            [dot_t(a[:, :half], x_ref[:half, :half]), dot_t(a, x_ref[half:, :])], axis=1
        )

        @pl.when(q == 0)
        def _():
            o_ref[sl, :] = p

        @pl.when(q != 0)
        def _():
            o_ref[sl, :] = o_ref[sl, :] - dot(p, pq[...])

        return carry

    lax.fori_loop(0, 2 * NB // rows, body, 0)

    @pl.when(r == 0)
    def _():
        @pl.when(q == 0)
        def _():
            for i in range(4):
                for j in range(4):
                    o_ref[B * i:B * i + B, B * j:B * j + B] = u_ref[B * j:B * j + B, B * i:B * i + B].T

        @pl.when(q != 0)
        def _():
            o_ref[:NB, :] = jnp.zeros((NB, NB), F32)


def update(kbuf, ap, aq, kernel):
    vmem = pltpu.VMEM
    return pl.pallas_call(
        update_kernel,
        out_shape=jax.ShapeDtypeStruct((2 * NB, NB), F32),
        in_specs=[pl.BlockSpec(memory_space=pl.ANY)] * 4,
        out_specs=pl.BlockSpec(memory_space=vmem),
        scratch_shapes=[
            vmem((KROWS, B), F32), vmem((2 * NB, NB), F32), vmem((NB, NB), F32),
            vmem((NB, NB), F32), vmem((NB, NB), F32), vmem((NB, NB), F32), vmem((NB, NB), F32),
            pltpu.SemaphoreType.DMA((4,)),
        ],
        name="update",
    )(kbuf, ap, aq, kernel)


def on_device(kernel):
    kbuf, ap, aq = distribute(kernel)
    return update(kbuf, ap, aq, kernel)


def solution(mesh):
    return jax.shard_map(
        on_device, mesh=mesh, in_specs=(P("row", "col"),), out_specs=P("row", "col"), check_vma=False
    )
```

profile of v0, /device:TPU:235, one launch (start us, length us, event | category | flops | bytes accessed | tf_op | source)
XLA Modules:
  0.0 114.7 jit_solution(1444069440692167234)
XLA Ops:
  0.0 84.2 %distribute.1 = (f32[1280,128]{1,0:T(8,128)}, f32[1024,512]{1,0:T(8,128)}, f32[512,512]{1,0:T(8,128)}) custom-call(f32[1024,512]{1,0:T(8,128)} %g_any.1), custom_call_target="tpu_custom_call" | custom-call | tf_op jit(solution)/shard_map/distribute/pallas_call | solution.py:406
  84.2 30.3 %update.1 = f32[1024,512]{1,0:T(8,128)} custom-call(f32[1280,128]{1,0:T(8,128)} %get-tuple-element.8.k_any, f32[1024,512]{1,0:T(8,128)} %get-tuple-element.9.a_any, f32[512,512]{1,0:T(8,128)} %get-tuple-element.10.q_any, f32[1024,512]{1,0:T(8,128)} %g_any.1), custom_call_target="tpu_custom_call" | custom-call | tf_op jit(solution)/shard_map/update/pallas_call | solution.py:484
where the time goes:
time: 115 us
  Pallas kernels  114 us (99%)
    pallas_call x1, Pallas kernels, distribute(): pl.pallas_call(comm_kernel, out_shape=[jax.ShapeDtypeStruct((KROWS, B), F...  84.2 us
    pallas_call x1, Pallas kernels, update(): pl.pallas_call(update_kernel, out_shape=jax.ShapeDtypeStruct((2 * NB, NB)...  30.3 us

commit v1 on v0

--- a/solution.py
+++ b/solution.py
@@ -27,11 +27,12 @@
 def sub(v, i):
     return jnp.broadcast_to(v[i:i + 1, :], (8, B))
 
-def micro(d, e):
+def micro(d, e, beside):
     n = len(d)
     iota = lax.broadcasted_iota(jnp.int32, (8, B), 0)
     us, vs = [], []
     for s in range(n):
+        beside(s)
         j0 = 8 * s
         cols = [lane(d[s], j0 + k) for k in range(8)]
         sp = {(i, k): sub(cols[k], i) for k in range(8) for i in range(k + 1)}
@@ -89,7 +90,7 @@
 def tdot(a, b):
     return lax.dot_general(a, b, (((0,), (0,)), ((), ())), precision=HI, preferred_element_type=F32)
 
-def factor(k_ref, u_ref, x_ref, w_ref):
+def factor(k_ref, u_ref, x_ref, w_ref, beside):
     for n, (i, j) in enumerate(UNITS):
         w_ref[B * i:B * i + B, B * j:B * j + B] = k_ref[B * n:B * n + B, :]
     x_ref[...] = jnp.zeros((NB, NB), F32)
@@ -100,7 +101,7 @@
         o = B * k
         d = [w_ref[o + 8 * t:o + 8 * t + 8, o:o + B] for t in range(16)]
         e = [jnp.where(col == row + 8 * t, 1.0, 0.0) for t in range(16)]
-        us, vs = micro(d, e)
+        us, vs = micro(d, e, lambda s, k=k: beside(k, s))
         for t in range(16):
             u_ref[o + 8 * t:o + 8 * t + 8, o:o + B] = jnp.where(col >= row + 8 * t, us[t], 0.0)
             x_ref[o + 8 * t:o + 8 * t + 8, o:o + B] = vs[t]
@@ -427,7 +428,7 @@
     )(kernel)
 
 
-def update_kernel(k_any, a_any, q_any, g_any, o_ref, kbuf, ap, aq, u_ref, x_ref, w_ref, pq, sems):
+def update_kernel(k_any, a_any, q_any, g_any, o_ref, kbuf, ap, aq, u_ref, x_ref, w_ref, pq, p_ref, sems):
     r = lax.axis_index("row")
     q = lax.axis_index("col")
     loads = [
@@ -437,22 +438,29 @@
     for cp in loads:
         cp.start()
     loads[0].wait()
-    factor(kbuf, u_ref, x_ref, w_ref)
-    loads[1].wait()
-    loads[2].wait()
+
+    def beside(k, s):
+        if k == 0:
+            return
+        if k == 1 and s == 0:
+            loads[1].wait()
+            loads[2].wait()
+        lo, hi = B * (k - 1), B * k
+        part = slice(64 * s, 64 * s + 64)
+        p_ref[part, lo:hi] = dot_t(ap[part, :hi], x_ref[lo:hi, :hi])
+        if s < 4:
+            cols = slice(B * s, B * s + B)
+            pq[lo:hi, cols] = dot(x_ref[lo:hi, :hi], aq[:hi, cols])
+
+    factor(kbuf, u_ref, x_ref, w_ref, beside)
     loads[3].wait()
-
-    half = NB // 2
-    pq[:half] = dot(x_ref[:half, :half], aq[:half, :])
-    pq[half:] = dot(x_ref[half:, :], aq[...])
+    last = NB - B
+    pq[last:] = dot(x_ref[last:, :], aq[...])
     rows = 256
 
     def body(n, carry):
         sl = pl.ds(pl.multiple_of(rows * n, rows), rows)
-        a = ap[sl, :]
-        p = jnp.concatenate(
-            [dot_t(a[:, :half], x_ref[:half, :half]), dot_t(a, x_ref[half:, :])], axis=1
-        )
+        p = jnp.concatenate([p_ref[sl, :last], dot_t(ap[sl, :], x_ref[last:, :])], axis=1)
 
         @pl.when(q == 0)
         def _():
@@ -489,7 +497,7 @@
         scratch_shapes=[
             vmem((KROWS, B), F32), vmem((2 * NB, NB), F32), vmem((NB, NB), F32),
             vmem((NB, NB), F32), vmem((NB, NB), F32), vmem((NB, NB), F32), vmem((NB, NB), F32),
-            pltpu.SemaphoreType.DMA((4,)),
+            vmem((2 * NB, NB), F32), pltpu.SemaphoreType.DMA((4,)),
         ],
         name="update",
     )(kbuf, ap, aq, kernel)

time: 115 us -> 116 us (level)
  no operation moved by 1% of the time
where the time goes in v1:
time: 116 us; the launch traced here: 115 us
  Pallas kernels  115 us (99%)
    pallas_call x1, Pallas kernels, distribute(): pl.pallas_call(comm_kernel, out_shape=[jax.ShapeDtypeStruct((KROWS, B), F...  84.2 us
    pallas_call x1, Pallas kernels, update(): pl.pallas_call(update_kernel, out_shape=jax.ShapeDtypeStruct((2 * NB, NB)...  31 us

profile of v1, /device:TPU:235, one launch (start us, length us, event | category | flops | bytes accessed | tf_op | source)
XLA Modules:
  0.0 115.4 jit_solution(6579444380912736398)
XLA Ops:
  0.0 84.2 %distribute.1 = (f32[1280,128]{1,0:T(8,128)}, f32[1024,512]{1,0:T(8,128)}, f32[512,512]{1,0:T(8,128)}) custom-call(f32[1024,512]{1,0:T(8,128)} %g_any.1), custom_call_target="tpu_custom_call" | custom-call | tf_op jit(solution)/shard_map/distribute/pallas_call | solution.py:407
  84.2 31.0 %update.1 = f32[1024,512]{1,0:T(8,128)} custom-call(f32[1280,128]{1,0:T(8,128)} %get-tuple-element.8.k_any, f32[1024,512]{1,0:T(8,128)} %get-tuple-element.9.a_any, f32[512,512]{1,0:T(8,128)} %get-tuple-element.10.q_any, f32[1024,512]{1,0:T(8,128)} %g_any.1), custom_call_target="tpu_custom_call" | custom-call | tf_op jit(solution)/shard_map/update/pallas_call | solution.py:492
